TPU v7x, 32 devices: a whole 2x2x4 slice. The times are simulated.
32 devices in a mesh: gx: 4 (over y, x), gy: 2 (over core), zt: 4 (over z).
Axes of the slice: x: 2, y: 2, z: 4, core: 2. Of those that a mesh axis runs over, the one named last changes fastest.
Arguments:
- links: float32 [4, 4, 8, 8, 4, 128], P(None, None, 'zt', 'gx', 'gy'), may hold values from -1 to 1, as said below
- trials: float32 [8, 4, 8, 8, 4, 128], P(None, None, 'zt', 'gx', 'gy'), may hold values from 0.02 to 0.98
- cos_polar: float32 [4, 8, 8, 4, 128], P(None, 'zt', 'gx', 'gy'), may hold values from -0.98 to 0.98
- azimuth: float32 [4, 8, 8, 4, 128], P(None, 'zt', 'gx', 'gy'), may hold values from -3.140625 to 3.140625
- accepted: int32 [4, 8, 8, 4, 128], P(None, 'zt', 'gx', 'gy'), may hold values from 0 to 7
Outputs:
- new_links: float32 [4, 4, 8, 8, 4, 128], P(None, None, 'zt', 'gx', 'gy')
- transporters: float32 [4, 8, 8, 4, 128], P(None, 'zt', 'gx', 'gy')
Inputs may be any that keep to these rules, and one draw needn't show every extreme that they name: `links`: every link is a unit quaternion: its four components' squares sum to one.
All inputs are finite; a program needn't handle non-finite values.
Results may differ from a plain program's by a relative error of at most 0.0003.
Values sent between devices are 32-bit elements; how exact they have to be, the bound alone decides.
A program may use at most 64 MiB of HBM per device.

v0:
```python
from functools import reduce

import jax
import jax.numpy as jnp
from jax import lax
from jax.sharding import PartitionSpec as P

plaq_weight = 5.0 / 3.0
rect_weight = -1.0 / 12.0
coupling = 1.5


def with_halo(shard, sides, width):
    for axis, dim in sides:
        size, length = (lax.axis_size(axis), shard.shape[dim])
        up = [(i, (i + 1) % size) for i in range(size)]
        down = [(j, i) for i, j in up]
        last = lax.slice_in_dim(shard, length - width, length, axis=dim)
        leading = lax.slice_in_dim(shard, 0, width, axis=dim)
        before = lax.ppermute(last, axis, up)
        after = lax.ppermute(leading, axis, down)
        shard = jnp.concatenate([before, shard, after], axis=dim)
    return shard


def entering(part, axis, combine, identity):
    place = lax.axis_index(axis)
    gathered = lax.all_gather(part, axis)
    state = jnp.zeros_like(part) + jnp.asarray(identity, part.dtype)

    def one(lap, state):
        return combine(state, lax.dynamic_index_in_dim(gathered, lap, 0, False))

    return lax.fori_loop(0, place, one, state)


def quat_mul(left, right):
    return jnp.stack(
        [
            left[0] * right[0] - left[1] * right[1] - left[2] * right[2] - left[3] * right[3],
            left[0] * right[1] + right[0] * left[1] - left[2] * right[3] + left[3] * right[2],
            left[0] * right[2] + right[0] * left[2] - left[3] * right[1] + left[1] * right[3],
            left[0] * right[3] + right[0] * left[3] - left[1] * right[2] + left[2] * right[1],
        ]
    )


def quat_conj(value):
    return jnp.concatenate([value[:1], -value[1:]], axis=0)


def chain_of(factors):
    return reduce(quat_mul, factors)


def staple_sum(lookup, along):
    plaq = 0.0
    rect = 0.0
    for across in range(4):
        if across == along:
            continue

        def link_at(direction, step_along, step_across):
            offset = tuple(
                (
                    (step_along if index == along else 0) + (step_across if index == across else 0)
                    for index in range(4)
                )
            )
            return lookup(direction, offset)

        def back_at(direction, step_along, step_across):
            return quat_conj(link_at(direction, step_along, step_across))

        plaq = plaq + chain_of([link_at(across, 1, 0), back_at(along, 0, 1), back_at(across, 0, 0)])
        plaq = plaq + chain_of(
            [back_at(across, 1, -1), back_at(along, 0, -1), link_at(across, 0, -1)]
        )
        rect = rect + chain_of(
            [
                link_at(along, 1, 0),
                link_at(across, 2, 0),
                back_at(along, 1, 1),
                back_at(along, 0, 1),
                back_at(across, 0, 0),
            ]
        )
        rect = rect + chain_of(
            [
                link_at(along, 1, 0),
                back_at(across, 2, -1),
                back_at(along, 1, -1),
                back_at(along, 0, -1),
                link_at(across, 0, -1),
            ]
        )
        rect = rect + chain_of(
            [
                link_at(across, 1, 0),
                back_at(along, 0, 1),
                back_at(along, -1, 1),
                back_at(across, -1, 0),
                link_at(along, -1, 0),
            ]
        )
        rect = rect + chain_of(
            [
                back_at(across, 1, -1),
                back_at(along, 0, -1),
                back_at(along, -1, -1),
                link_at(across, -1, -1),
                link_at(along, -1, 0),
            ]
        )
        rect = rect + chain_of(
            [
                link_at(across, 1, 0),
                link_at(across, 1, 1),
                back_at(along, 0, 2),
                back_at(across, 0, 1),
                back_at(across, 0, 0),
            ]
        )
        rect = rect + chain_of(
            [
                back_at(across, 1, -1),
                back_at(across, 1, -2),
                back_at(along, 0, -2),
                link_at(across, 0, -2),
                link_at(across, 0, -1),
            ]
        )
    return plaq_weight * plaq + rect_weight * rect


def pick_trials(trials, accepted):
    numbers = jnp.arange(trials.shape[0], dtype=jnp.int32).reshape(-1, 1, 1, 1, 1, 1)
    return jnp.sum(jnp.where(accepted[None] == numbers, trials, jnp.float32(0.0)), axis=0)


def even_sites(t_start, x_start, y_start, shape):
    total = t_start + lax.broadcasted_iota(jnp.int32, shape, 0)
    total = total + x_start + lax.broadcasted_iota(jnp.int32, shape, 1)
    total = total + y_start + lax.broadcasted_iota(jnp.int32, shape, 2)
    total = total + lax.broadcasted_iota(jnp.int32, shape, 3)
    return total % 2 == 0


def heat_bath(old_link, staple, draw, cos_value, azimuth, even):
    size = jnp.sqrt(jnp.sum(staple * staple, axis=0))
    floor = jnp.maximum(size, 1.0)
    strength = coupling * floor
    low = jnp.exp(-2.0 * strength)
    head = 1.0 + jnp.log(low + (1.0 - low) * draw) / strength
    radius = jnp.sqrt(1.0 - head * head)
    side = jnp.sqrt(1.0 - cos_value * cos_value)
    trial = jnp.stack(
        [
            head,
            radius * side * jnp.cos(azimuth),
            radius * side * jnp.sin(azimuth),
            radius * cos_value,
        ]
    )
    updated = quat_mul(trial, quat_conj(staple)) / floor[None]
    return jnp.where(even[None], updated, old_link)


def staple_for(padded, along, t_len, x_len, y_len):
    memo = {}

    def lookup(direction, offset):
        keyname = (direction, offset)
        if keyname not in memo:
            piece = padded[
                direction,
                :,
                2 + offset[0] : 2 + offset[0] + t_len,
                2 + offset[1] : 2 + offset[1] + x_len,
                2 + offset[2] : 2 + offset[2] + y_len,
                :,
            ]
            memo[keyname] = jnp.roll(piece, -offset[3], axis=4)
        return memo[keyname]

    return staple_sum(lookup, along)


def local(links, trials, cos_polar, azimuth, accepted):
    t_len = links.shape[2]
    x_len = links.shape[3]
    y_len = links.shape[4]
    padded = with_halo(links, (("gx", 3), ("gy", 4), ("zt", 2)), 2)
    even = even_sites(
        lax.axis_index("zt") * t_len,
        lax.axis_index("gx") * x_len,
        lax.axis_index("gy") * y_len,
        links.shape[2:],
    )
    picked = pick_trials(trials, accepted)
    new_links = jnp.stack(
        [
            heat_bath(
                links[direction],
                staple_for(padded, direction, t_len, x_len, y_len),
                picked[direction],
                cos_polar[direction],
                azimuth[direction],
                even,
            )
            for direction in range(4)
        ]
    )
    inner = lax.associative_scan(quat_mul, new_links[0], axis=1)
    total = inner[:, -1]
    identity = jnp.concatenate([jnp.ones_like(total[:1]), jnp.zeros_like(total[1:])], axis=0)
    before = entering(total, "zt", quat_mul, identity)
    transporters = quat_mul(before[:, None], inner)
    return (new_links, transporters)


def solution(mesh):
    return jax.shard_map(
        local,
        mesh=mesh,
        in_specs=(
            P(None, None, "zt", "gx", "gy", None),
            P(None, None, "zt", "gx", "gy", None),
            P(None, "zt", "gx", "gy", None),
            P(None, "zt", "gx", "gy", None),
            P(None, "zt", "gx", "gy", None),
        ),
        out_specs=(P(None, None, "zt", "gx", "gy", None), P(None, "zt", "gx", "gy", None)),
        check_vma=False,
    )
```

profile of v0, /device:TPU:0, one launch (start us, length us, event | category | flops | bytes accessed | tf_op | source)
XLA Modules:
  0.0 130.4 jit_solution(7359237740833732547)
XLA Ops:
  0.7 3.0 %collective-permute-start = (f32[4,4,2,2,2,128]{5,4,3,2,1,0:T(2,128)}, f32[4,4,2,2,2,128]{5,4,3,2,1,0:T(2,128)S(1)}, u32[]{:S(2)}, u32[]{:S(2)}) collective-permute-start(f32[4,4,2,2,2,128]{5,4,3,2,1,0:T(2,128)} %param.7), channel_id=1, source_target_pairs={{0,8},{8,16},{16,24},{24,0},{1,9},{9,17},{17,25},{25,1},{2,10},{10... | collective-permute-start | bytes 196616 | tf_op jit(solution)/shard_map/ppermute | solution.py:20
  3.7 1.0 collective-permute-start.1
  4.7 0.8 slice_negate_fusion.44
  5.5 0.8 slice_bitcast_fusion.12
  8.5 0.7 slice.5073
  17.2 0.7 fusion.944
  23.0 4.1 %collective-permute-start.4 = (f32[4,4,2,6,6,128]{5,1,4,3,2,0:T(4,128)S(1)}, f32[4,4,2,6,6,128]{5,1,4,3,2,0:T(4,128)S(1)}, u32[]{:S(2)}, u32[]{:S(2)}) collective-permute-start(f32[4,4,2,6,6,128]{5,1,4,3,2,0:T(4,128)S(1)} %copy_dynamic-update-slice_fusion.1), channel_id=1, source_target_pairs={{1,0},{2,1},{3,2},{0,3},{5,4},{6,5},{7,6},{4,7},{9,8},{10,9},{11,1... | collective-permute-start | bytes 1769480 | tf_op jit(solution)/shard_map/ppermute | solution.py:21
  30.1 0.7 fusion.91
  30.8 0.7 fusion.131
  31.6 0.7 fusion.836
  33.2 0.7 multiply_subtract_fusion.74
  39.3 0.7 maximum_negate_fusion.3
  40.1 0.7 collective-permute-done.4
  41.3 0.7 slice_negate_fusion.38
  42.1 11.4 %collective-permute-done.5 = f32[4,4,2,6,6,128]{5,1,4,3,2,0:T(4,128)S(1)} collective-permute-done((f32[4,4,2,6,6,128]{5,1,4,3,2,0:T(4,128)S(1)}, f32[4,4,2,6,6,128]{5,1,4,3,2,0:T(4,128)S(1)}, u32[]{:S(2)}, u32[]{:S(2)}) %collective-permute-start.5) | collective-permute-done | bytes 589856 | tf_op jit(solution)/shard_map/ppermute | solution.py:20
  55.8 0.7 fusion.584
  62.2 0.7 multiply_subtract_fusion.58
  67.4 0.7 multiply_subtract_fusion.47
  68.2 0.7 multiply_subtract_fusion.27
  79.8 0.7 multiply_subtract_fusion.75
  81.2 0.7 multiply_subtract_fusion.8
  89.5 0.8 multiply_subtract_fusion.186
  91.2 13.1 %all-gather = f32[16,1,2,2,128]{4,3,2,1,0:T(2,128)S(1)} all-gather(f32[4,1,2,2,128]{4,3,2,1,0:T(2,128)S(1)} %slice.5720), channel_id=2, replica_groups=mesh['gx'=4,'gy'=2,'zt'=4] {'zt'}, dimensions={0}, use_global_device_ids=true | all-gather | bytes 40960 | tf_op jit(solution)/shard_map/all_gather | solution.py:28
  104.7 0.7 fusion.587
  105.4 0.7 fusion.551
  106.2 0.7 multiply_add_fusion.360
  107.6 0.8 multiply_subtract_fusion.38
  108.4 0.8 multiply_subtract_fusion.35
  109.2 0.8 multiply_subtract_fusion.18
  110.1 0.8 multiply_add_fusion.180
  110.8 0.8 fusion.596
  111.6 0.8 multiply_subtract_fusion.45
  112.5 0.7 multiply_add_fusion.141
  113.3 0.7 multiply_add_fusion.120
  114.0 0.7 fusion.956
  114.8 0.7 multiply_add_fusion.111
  115.6 0.7 multiply_add_fusion.60
  116.3 0.7 fusion.848
  117.0 0.8 multiply_subtract_fusion.85
  117.9 0.8 multiply_subtract_fusion.6
  118.8 0.7 multiply_add_fusion.24
  119.6 1.4 %multiply_reduce_fusion = (f32[2,2,2,128]{3,2,1,0:T(2,128)S(1)}, f32[4,2,2,2,128]{4,3,2,1,0:T(2,128)S(1)}) fusion(f32[1,2,2,2,128]{4,3,2,1,0:T(2,128)} %get-tuple-element.1650, f32[1,2,2,2,128]{4,3,2,1,0:T(2,128)} %get-tuple-element.1651, f32[1,2,2,2,128]{4,3,2,1,0:T(2,128)} %get-tuple-element.1652, f32[1,2,2,2,128]{4,3,2,1,0:T(2,128)} %get-tuple-element.1671, ...), kind=kLoop, calls=%fused_computation.228 | loop fusion | flops 404480 | bytes 413696 | tf_op jit(solution)/shard_map/reduce_sum | solution.py:150
  121.1 0.7 multiply_add_fusion.351
  121.9 0.7 fusion.560
  123.5 0.7 fusion.752
  124.3 0.8 multiply_add_fusion.246
  125.2 1.2 multiply_reduce_fusion.1
  126.9 0.8 add_bitcast_fusion.8
  (681 shorter events, 60.6 us)
Async XLA Ops:
  0.7 10.4 %collective-permute-start = (f32[4,4,2,2,2,128]{5,4,3,2,1,0:T(2,128)}, f32[4,4,2,2,2,128]{5,4,3,2,1,0:T(2,128)S(1)}, u32[]{:S(2)}, u32[]{:S(2)}) collective-permute-start(f32[4,4,2,2,2,128]{5,4,3,2,1,0:T(2,128)} %param.7), channel_id=1, source_target_pairs={{0,8},{8,16},{16,24},{24,0},{1,9},{9,17},{17,25},{25,1},{2,10},{10... | collective-permute-start | bytes 196616 | tf_op jit(solution)/shard_map/ppermute | solution.py:20
  3.7 7.5 %collective-permute-start.1 = (f32[4,4,2,2,2,128]{5,4,3,2,1,0:T(2,128)}, f32[4,4,2,2,2,128]{5,4,3,2,1,0:T(2,128)S(1)}, u32[]{:S(2)}, u32[]{:S(2)}) collective-permute-start(f32[4,4,2,2,2,128]{5,4,3,2,1,0:T(2,128)} %param.7), channel_id=1, source_target_pairs={{8,0},{16,8},{24,16},{0,24},{9,1},{17,9},{25,17},{1,25},{10,2},{18... | collective-permute-start | bytes 196616 | tf_op jit(solution)/shard_map/ppermute | solution.py:21
  8.4 24.0 %copy-start.24 = (f32[4,2,2,2,2]{4,3,2,1,0:T(2,128)}, f32[4,2,2,2,2]{4,3,2,1,0:T(2,128)S(1)}, u32[]{:S(2)}) copy-start(f32[4,2,2,2,2]{4,3,2,1,0:T(2,128)S(1)} %get-tuple-element.1775) | copy-start | bytes 772
  8.5 23.9 %copy-start.26 = (f32[4,2,2,2,126]{4,3,2,1,0:T(2,128)}, f32[4,2,2,2,126]{4,3,2,1,0:T(2,128)S(1)}, u32[]{:S(2)}) copy-start(f32[4,2,2,2,126]{4,3,2,1,0:T(2,128)S(1)} %get-tuple-element.1777) | copy-start | bytes 48388
  9.7 53.9 %copy-start.4 = (f32[3,2,2,2,128]{4,3,2,1,0:T(2,128)}, f32[3,2,2,2,128]{4,3,2,1,0:T(2,128)S(1)}, u32[]{:S(2)}) copy-start(f32[3,2,2,2,128]{4,3,2,1,0:T(2,128)S(1)} %maximum_negate_fusion.15) | copy-start | bytes 36868
  10.0 17.8 %copy-start.53 = (f32[3,2,2,2,128]{4,3,2,1,0:T(2,128)}, f32[3,2,2,2,128]{4,3,2,1,0:T(2,128)S(1)}, u32[]{:S(2)}) copy-start(f32[3,2,2,2,128]{4,3,2,1,0:T(2,128)S(1)} %maximum_negate_fusion.5) | copy-start | bytes 36868
  10.1 79.3 %copy-start.76 = (f32[4,2,2,2,128]{4,3,2,1,0:T(2,128)}, f32[4,2,2,2,128]{4,3,2,1,0:T(2,128)S(1)}, u32[]{:S(2)}) copy-start(f32[4,2,2,2,128]{4,3,2,1,0:T(2,128)S(1)} %fusion) | copy-start | bytes 49156
  11.2 11.5 %collective-permute-start.2 = (f32[4,4,2,6,2,128]{5,4,3,2,1,0:T(2,128)S(1)}, f32[4,4,2,6,2,128]{5,4,3,2,1,0:T(2,128)S(1)}, u32[]{:S(2)}, u32[]{:S(2)}) collective-permute-start(f32[4,4,2,6,2,128]{5,4,3,2,1,0:T(2,128)S(1)} %get-tuple-element.1260), channel_id=1, source_target_pairs={{0,4},{4,0},{1,5},{5,1},{2,6},{6,2},{3,7},{7,3},{8,12},{12,8},{9,1... | collective-permute-start | bytes 589832 | tf_op jit(solution)/shard_map/ppermute | solution.py:20
  11.3 11.6 %collective-permute-start.3 = (f32[4,4,2,6,2,128]{5,4,3,2,1,0:T(2,128)S(1)}, f32[4,4,2,6,2,128]{5,4,3,2,1,0:T(2,128)S(1)}, u32[]{:S(2)}, u32[]{:S(2)}) collective-permute-start(f32[4,4,2,6,2,128]{5,4,3,2,1,0:T(2,128)S(1)} %get-tuple-element.1260), channel_id=1, source_target_pairs={{4,0},{0,4},{5,1},{1,5},{6,2},{2,6},{7,3},{3,7},{12,8},{8,12},{13,... | collective-permute-start | bytes 589832 | tf_op jit(solution)/shard_map/ppermute | solution.py:21
  12.1 51.2 %copy-start.6 = (f32[1,3,2,2,2,128]{5,4,3,2,1,0:T(2,128)}, f32[1,3,2,2,2,128]{5,4,3,2,1,0:T(2,128)S(1)}, u32[]{:S(2)}) copy-start(f32[1,3,2,2,2,128]{5,4,3,2,1,0:T(2,128)S(1)} %get-tuple-element.1103) | copy-start | bytes 36868
  12.4 21.5 %copy-start.48 = (f32[1,3,2,2,2,128]{5,4,3,2,1,0:T(2,128)}, f32[1,3,2,2,2,128]{5,4,3,2,1,0:T(2,128)S(1)}, u32[]{:S(2)}) copy-start(f32[1,3,2,2,2,128]{5,4,3,2,1,0:T(2,128)S(1)} %get-tuple-element.1099) | copy-start | bytes 36868
  23.0 17.8 %collective-permute-start.4 = (f32[4,4,2,6,6,128]{5,1,4,3,2,0:T(4,128)S(1)}, f32[4,4,2,6,6,128]{5,1,4,3,2,0:T(4,128)S(1)}, u32[]{:S(2)}, u32[]{:S(2)}) collective-permute-start(f32[4,4,2,6,6,128]{5,1,4,3,2,0:T(4,128)S(1)} %copy_dynamic-update-slice_fusion.1), channel_id=1, source_target_pairs={{1,0},{2,1},{3,2},{0,3},{5,4},{6,5},{7,6},{4,7},{9,8},{10,9},{11,1... | collective-permute-start | bytes 1769480 | tf_op jit(solution)/shard_map/ppermute | solution.py:21
  27.1 26.4 %collective-permute-start.5 = (f32[4,4,2,6,6,128]{5,1,4,3,2,0:T(4,128)S(1)}, f32[4,4,2,6,6,128]{5,1,4,3,2,0:T(4,128)S(1)}, u32[]{:S(2)}, u32[]{:S(2)}) collective-permute-start(f32[4,4,2,6,6,128]{5,1,4,3,2,0:T(4,128)S(1)} %copy_dynamic-update-slice_fusion.1), channel_id=1, source_target_pairs={{0,1},{1,2},{2,3},{3,0},{4,5},{5,6},{6,7},{7,4},{8,9},{9,10},{10,1... | collective-permute-start | bytes 1769480 | tf_op jit(solution)/shard_map/ppermute | solution.py:20
  27.4 11.9 %copy-start.2 = (f32[4,2,2,2,127]{4,3,2,1,0:T(2,128)}, f32[4,2,2,2,127]{4,3,2,1,0:T(2,128)S(1)}, u32[]{:S(2)}) copy-start(f32[4,2,2,2,127]{4,3,2,1,0:T(2,128)S(1)} %get-tuple-element.1770) | copy-start | bytes 48772
  31.6 31.9 %copy-start.12 = (f32[1,3,2,2,2,128]{5,4,3,2,1,0:T(2,128)}, f32[1,3,2,2,2,128]{5,4,3,2,1,0:T(2,128)S(1)}, u32[]{:S(2)}) copy-start(f32[1,3,2,2,2,128]{5,4,3,2,1,0:T(2,128)S(1)} %get-tuple-element.1002) | copy-start | bytes 36868
  42.1 13.0 %copy-start.60 = (f32[1,3,2,2,2,128]{5,4,3,2,1,0:T(2,128)}, f32[1,3,2,2,2,128]{5,4,3,2,1,0:T(2,128)S(1)}, u32[]{:S(2)}) copy-start(f32[1,3,2,2,2,128]{5,4,3,2,1,0:T(2,128)S(1)} %get-tuple-element.1852) | copy-start | bytes 36868
  42.1 13.7 %copy-start.51 = (f32[1,3,2,2,2,128]{5,4,3,2,1,0:T(2,128)}, f32[1,3,2,2,2,128]{5,4,3,2,1,0:T(2,128)S(1)}, u32[]{:S(2)}) copy-start(f32[1,3,2,2,2,128]{5,4,3,2,1,0:T(2,128)S(1)} %get-tuple-element.1854) | copy-start | bytes 36868
  42.1 21.1 %copy-start.10 = (f32[1,3,2,2,2,128]{5,4,3,2,1,0:T(2,128)}, f32[1,3,2,2,2,128]{5,4,3,2,1,0:T(2,128)S(1)}, u32[]{:S(2)}) copy-start(f32[1,3,2,2,2,128]{5,4,3,2,1,0:T(2,128)S(1)} %get-tuple-element.1851) | copy-start | bytes 36868
  42.1 21.9 %copy-start.58 = (f32[1,3,2,2,2,128]{5,4,3,2,1,0:T(2,128)}, f32[1,3,2,2,2,128]{5,4,3,2,1,0:T(2,128)S(1)}, u32[]{:S(2)}) copy-start(f32[1,3,2,2,2,128]{5,4,3,2,1,0:T(2,128)S(1)} %get-tuple-element.1853) | copy-start | bytes 36868
  54.2 25.3 %copy-start.63 = (f32[1,2,2,2,128]{4,3,2,1,0:T(2,128)}, f32[1,2,2,2,128]{4,3,2,1,0:T(2,128)S(1)}, u32[]{:S(2)}) copy-start(f32[1,2,2,2,128]{4,3,2,1,0:T(2,128)S(1)} %get-tuple-element.53) | copy-start | bytes 12292
  55.7 23.9 %copy-start.78 = (f32[1,2,2,2,128]{4,3,2,1,0:T(2,128)}, f32[1,2,2,2,128]{4,3,2,1,0:T(2,128)S(1)}, u32[]{:S(2)}) copy-start(f32[1,2,2,2,128]{4,3,2,1,0:T(2,128)S(1)} %get-tuple-element.69) | copy-start | bytes 12292
  77.2 12.3 %copy-start.62 = (f32[4,2,2,2,128]{4,3,2,1,0:T(2,128)}, f32[4,2,2,2,128]{4,3,2,1,0:T(2,128)S(1)}, u32[]{:S(2)}) copy-start(f32[4,2,2,2,128]{4,3,2,1,0:T(2,128)S(1)} %get-tuple-element.250) | copy-start | bytes 49156
  77.2 12.3 %copy-start.86 = (f32[2,2,2,128]{3,2,1,0:T(2,128)}, f32[2,2,2,128]{3,2,1,0:T(2,128)S(1)}, u32[]{:S(2)}) copy-start(f32[2,2,2,128]{3,2,1,0:T(2,128)S(1)} %get-tuple-element.249) | copy-start | bytes 12292
  77.2 12.3 %copy-start.43 = (f32[3,2,2,2,128]{4,3,2,1,0:T(2,128)}, f32[3,2,2,2,128]{4,3,2,1,0:T(2,128)S(1)}, u32[]{:S(2)}) copy-start(f32[3,2,2,2,128]{4,3,2,1,0:T(2,128)S(1)} %slice_negate_fusion.16) | copy-start | bytes 36868
  79.7 24.6 %copy-start.1 = (f32[4,2,2,128]{3,2,1,0:T(2,128)S(1)}, f32[4,2,2,128]{3,2,1,0:T(2,128)}, u32[]{:S(2)}) copy-start(f32[4,2,2,128]{3,2,1,0:T(2,128)} %constant.54.clone.1) | copy-start | bytes 24580
  83.2 25.2 %copy-start.23 = (f32[4,2,2,2,126]{4,3,2,1,0:T(2,128)S(1)}, f32[4,2,2,2,126]{4,3,2,1,0:T(2,128)}, u32[]{:S(2)}) copy-start(f32[4,2,2,2,126]{4,3,2,1,0:T(2,128)} %copy-done.22) | copy-start | bytes 48388
  85.8 27.4 %copy-start.11 = (f32[1,3,2,2,2,128]{5,4,3,2,1,0:T(2,128)S(1)}, f32[1,3,2,2,2,128]{5,4,3,2,1,0:T(2,128)}, u32[]{:S(2)}) copy-start(f32[1,3,2,2,2,128]{5,4,3,2,1,0:T(2,128)} %copy-done.10) | copy-start | bytes 36868
  87.8 27.7 %copy-start.9 = (f32[1,3,2,2,2,128]{5,4,3,2,1,0:T(2,128)S(1)}, f32[1,3,2,2,2,128]{5,4,3,2,1,0:T(2,128)}, u32[]{:S(2)}) copy-start(f32[1,3,2,2,2,128]{5,4,3,2,1,0:T(2,128)} %copy-done.8) | copy-start | bytes 36868
  89.1 28.0 %copy-start.3 = (f32[4,2,2,2,127]{4,3,2,1,0:T(2,128)S(1)}, f32[4,2,2,2,127]{4,3,2,1,0:T(2,128)}, u32[]{:S(2)}) copy-start(f32[4,2,2,2,127]{4,3,2,1,0:T(2,128)} %copy-done.2) | copy-start | bytes 48772
  89.1 28.8 %copy-start.66 = (f32[1,2,2,2,128]{4,3,2,1,0:T(2,128)S(1)}, f32[1,2,2,2,128]{4,3,2,1,0:T(2,128)}, u32[]{:S(2)}) copy-start(f32[1,2,2,2,128]{4,3,2,1,0:T(2,128)} %copy-done.65) | copy-start | bytes 12292
  89.1 30.4 %copy-start.13 = (f32[1,3,2,2,2,128]{5,4,3,2,1,0:T(2,128)S(1)}, f32[1,3,2,2,2,128]{5,4,3,2,1,0:T(2,128)}, u32[]{:S(2)}) copy-start(f32[1,3,2,2,2,128]{5,4,3,2,1,0:T(2,128)} %copy-done.12) | copy-start | bytes 36868
  90.3 14.0 %copy-start.88 = (f32[1,2,2,2,128]{4,3,2,1,0:T(2,128)}, f32[1,2,2,2,128]{4,3,2,1,0:T(2,128)S(1)}, u32[]{:S(2)}) copy-start(f32[1,2,2,2,128]{4,3,2,1,0:T(2,128)S(1)} %get-tuple-element.34) | copy-start | bytes 12292
  104.3 18.3 %copy-start.64 = (f32[1,2,2,2,128]{4,3,2,1,0:T(2,128)S(1)}, f32[1,2,2,2,128]{4,3,2,1,0:T(2,128)}, u32[]{:S(2)}) copy-start(f32[1,2,2,2,128]{4,3,2,1,0:T(2,128)} %copy-done.63) | copy-start | bytes 12292
  104.6 16.5 %copy-start.59 = (f32[1,3,2,2,2,128]{5,4,3,2,1,0:T(2,128)S(1)}, f32[1,3,2,2,2,128]{5,4,3,2,1,0:T(2,128)}, u32[]{:S(2)}) copy-start(f32[1,3,2,2,2,128]{5,4,3,2,1,0:T(2,128)} %copy-done.58) | copy-start | bytes 36868
  104.6 17.3 %copy-start.61 = (f32[1,3,2,2,2,128]{5,4,3,2,1,0:T(2,128)S(1)}, f32[1,3,2,2,2,128]{5,4,3,2,1,0:T(2,128)}, u32[]{:S(2)}) copy-start(f32[1,3,2,2,2,128]{5,4,3,2,1,0:T(2,128)} %copy-done.60) | copy-start | bytes 36868
  104.6 18.0 %copy-start.56 = (f32[1,3,2,2,2,128]{5,4,3,2,1,0:T(2,128)S(1)}, f32[1,3,2,2,2,128]{5,4,3,2,1,0:T(2,128)}, u32[]{:S(2)}) copy-start(f32[1,3,2,2,2,128]{5,4,3,2,1,0:T(2,128)} %get-tuple-element.965) | copy-start | bytes 36868
  104.6 18.0 %copy-start.118 = (f32[1,1,2,2,2,128]{5,4,3,2,1,0:T(2,128)S(1)}, f32[1,1,2,2,2,128]{5,4,3,2,1,0:T(2,128)}, u32[]{:S(2)}) copy-start(f32[1,1,2,2,2,128]{5,4,3,2,1,0:T(2,128)} %get-tuple-element.464) | copy-start | bytes 12292
  104.6 18.2 %copy-start.55 = (f32[1,3,2,2,2,128]{5,4,3,2,1,0:T(2,128)S(1)}, f32[1,3,2,2,2,128]{5,4,3,2,1,0:T(2,128)}, u32[]{:S(2)}) copy-start(f32[1,3,2,2,2,128]{5,4,3,2,1,0:T(2,128)} %get-tuple-element.1003) | copy-start | bytes 36868
  104.6 18.2 %copy-start.87 = (f32[1,1,2,2,2,128]{5,4,3,2,1,0:T(2,128)S(1)}, f32[1,1,2,2,2,128]{5,4,3,2,1,0:T(2,128)}, u32[]{:S(2)}) copy-start(f32[1,1,2,2,2,128]{5,4,3,2,1,0:T(2,128)} %get-tuple-element.384) | copy-start | bytes 12292
  104.7 18.3 %copy-start.49 = (f32[1,3,2,2,2,128]{5,4,3,2,1,0:T(2,128)S(1)}, f32[1,3,2,2,2,128]{5,4,3,2,1,0:T(2,128)}, u32[]{:S(2)}) copy-start(f32[1,3,2,2,2,128]{5,4,3,2,1,0:T(2,128)} %copy-done.48) | copy-start | bytes 36868
  105.4 17.6 %copy-start.57 = (f32[1,3,2,2,2,128]{5,4,3,2,1,0:T(2,128)S(1)}, f32[1,3,2,2,2,128]{5,4,3,2,1,0:T(2,128)}, u32[]{:S(2)}) copy-start(f32[1,3,2,2,2,128]{5,4,3,2,1,0:T(2,128)} %get-tuple-element.1005) | copy-start | bytes 36868
  105.4 17.6 %copy-start.84 = (f32[1,3,2,2,2,128]{5,4,3,2,1,0:T(2,128)S(1)}, f32[1,3,2,2,2,128]{5,4,3,2,1,0:T(2,128)}, u32[]{:S(2)}) copy-start(f32[1,3,2,2,2,128]{5,4,3,2,1,0:T(2,128)} %get-tuple-element.1044) | copy-start | bytes 36868
  109.2 13.4 %copy-start.119 = (f32[1,1,2,2,2,128]{5,4,3,2,1,0:T(2,128)S(1)}, f32[1,1,2,2,2,128]{5,4,3,2,1,0:T(2,128)}, u32[]{:S(2)}) copy-start(f32[1,1,2,2,2,128]{5,4,3,2,1,0:T(2,128)} %get-tuple-element.465) | copy-start | bytes 12292
  111.6 11.6 %copy-start.7 = (f32[1,3,2,2,2,128]{5,4,3,2,1,0:T(2,128)S(1)}, f32[1,3,2,2,2,128]{5,4,3,2,1,0:T(2,128)}, u32[]{:S(2)}) copy-start(f32[1,3,2,2,2,128]{5,4,3,2,1,0:T(2,128)} %copy-done.6) | copy-start | bytes 36868
  112.5 10.7 %copy-start.46 = (f32[1,3,2,2,2,128]{5,4,3,2,1,0:T(2,128)S(1)}, f32[1,3,2,2,2,128]{5,4,3,2,1,0:T(2,128)}, u32[]{:S(2)}) copy-start(f32[1,3,2,2,2,128]{5,4,3,2,1,0:T(2,128)} %get-tuple-element.1245) | copy-start | bytes 36868
  112.5 10.7 %copy-start.83 = (f32[1,1,2,2,2,128]{5,4,3,2,1,0:T(2,128)S(1)}, f32[1,1,2,2,2,128]{5,4,3,2,1,0:T(2,128)}, u32[]{:S(2)}) copy-start(f32[1,1,2,2,2,128]{5,4,3,2,1,0:T(2,128)} %copy-done.82) | copy-start | bytes 12292
  112.5 10.7 %copy-start.85 = (f32[1,3,2,2,2,128]{5,4,3,2,1,0:T(2,128)S(1)}, f32[1,3,2,2,2,128]{5,4,3,2,1,0:T(2,128)}, u32[]{:S(2)}) copy-start(f32[1,3,2,2,2,128]{5,4,3,2,1,0:T(2,128)} %get-tuple-element.1006) | copy-start | bytes 36868
  112.5 10.7 %copy-start.115 = (f32[1,1,2,2,2,128]{5,4,3,2,1,0:T(2,128)S(1)}, f32[1,1,2,2,2,128]{5,4,3,2,1,0:T(2,128)}, u32[]{:S(2)}) copy-start(f32[1,1,2,2,2,128]{5,4,3,2,1,0:T(2,128)} %get-tuple-element.1016) | copy-start | bytes 12292
  (95 other events, 498.8 us)
where the time goes:
time: 132 us; the launch traced here: 130 us
  other arithmetic  84.3 us (64%)
  blocking collectives  13.1 us (10%)
  waiting for transfers between devices  12.1 us (9%)
  starting transfers between devices  8.68 us (7%)
  local copies, waits for them, and re-layouts  7.73 us (6%)
  between operations  4.27 us (3%)
    sub x152, other arithmetic, quat_mul(): left[0] * right[0] - left[1] * right[1] - left[2] * right[2]  38.4 us
    add x126, other arithmetic, quat_mul(): left[0] * right[1] + right[0] * left[1] - left[2] * right[3]  24.9 us
    all_gather x1, blocking collectives, entering(): gathered = lax.all_gather(part, axis)  13.1 us
    ppermute x3, waiting for transfers between devices, with_halo(): before = lax.ppermute(last, axis, up)  11.4 us
    neg x69, other arithmetic, quat_conj(): return jnp.concatenate([value[:1], -value[1:]], axis=0)  10.8 us
    ppermute x3, starting transfers between devices, with_halo(): after = lax.ppermute(leading, axis, down)  5.59 us
    slice x41, local copies, waits for them, and re-layouts, lookup(): memo[keyname] = jnp.roll(piece, -offset[3], axis=4)  5.19 us
    reduce_sum x4, other arithmetic, heat_bath(): size = jnp.sqrt(jnp.sum(staple * staple, axis=0))  3.23 us
  transfers between devices with their start and end apart: 6, of which 2 were waited for; matrix products, arithmetic and copies ran while one was open for 24% of the time, Pallas kernels for 0%

commit v1 on v0

v1 whole, which is shorter than its diff:
```python
import itertools

import jax
import jax.numpy as jnp
from jax import lax
from jax.experimental import pallas as pl
from jax.experimental.pallas import tpu as pltpu
from jax.sharding import PartitionSpec as P

plaq_weight = 5.0 / 3.0
rect_weight = -1.0 / 12.0
coupling = 1.5

MESH = pl.DeviceIdType.MESH
AXES = ("zt", "gx", "gy")
BITS = (4, 2, 1)


class Quat:
    def __init__(self, parts, flip=False):
        self.parts = tuple(parts)
        self.flip = flip

    def conj(self):
        return Quat(self.parts, not self.flip)

    def __mul__(self, other):
        if self.flip and other.flip:
            return (other.conj() * self.conj()).conj()
        a0, a1, a2, a3 = self.parts
        b0, b1, b2, b3 = other.parts
        if not self.flip and not other.flip:
            return Quat(
                (
                    (a0 * b0 - a1 * b1) - (a2 * b2 + a3 * b3),
                    (a0 * b1 + b0 * a1) - (a2 * b3 - a3 * b2),
                    (a0 * b2 + b0 * a2) - (a3 * b1 - a1 * b3),
                    (a0 * b3 + b0 * a3) - (a1 * b2 - a2 * b1),
                )
            )
        real = (a0 * b0 + a1 * b1) + (a2 * b2 + a3 * b3)
        if other.flip:
            return Quat(
                (
                    real,
                    (b0 * a1 - a0 * b1) + (a2 * b3 - a3 * b2),
                    (b0 * a2 - a0 * b2) + (a3 * b1 - a1 * b3),
                    (b0 * a3 - a0 * b3) + (a1 * b2 - a2 * b1),
                )
            )
        return Quat(
            (
                real,
                (a0 * b1 - b0 * a1) + (a2 * b3 - a3 * b2),
                (a0 * b2 - b0 * a2) + (a3 * b1 - a1 * b3),
                (a0 * b3 - b0 * a3) + (a1 * b2 - a2 * b1),
            )
        )

    def plain(self):
        if not self.flip:
            return self.parts
        return (self.parts[0],) + tuple(-part for part in self.parts[1:])

    def scaled(self, factor):
        return Quat(tuple(part * factor for part in self.parts), self.flip)

    def __add__(self, other):
        if self.flip == other.flip:
            return Quat(tuple(p + q for p, q in zip(self.parts, other.parts)), self.flip)
        (a0, a1, a2, a3), (b0, b1, b2, b3) = self.parts, other.parts
        return Quat((a0 + b0, a1 - b1, a2 - b2, a3 - b3), self.flip)


def canonical(offset, sizes):
    return tuple(1 if (step == -1 and size == 2) else step for step, size in zip(offset, sizes))


def halo_slots(sizes):
    slots = []
    for offset in itertools.product((0, 1, -1), repeat=3):
        used = [axis for axis in range(3) if offset[axis]]
        key = canonical(offset, sizes)
        if len(used) in (1, 2) and key not in slots:
            slots.append(key)
    return slots


def pieces_of(offset):
    used = [axis for axis in range(3) if offset[axis]]
    if len(used) == 1:
        return ((0, 4),)
    low, high = used
    if high == low + 1:
        return ((low, high + 1),)
    return ((low, low + 1), (high, high + 1))


def copies_of(sizes):
    slots = halo_slots(sizes)
    plan = [(slot, piece) for slot in slots for piece in pieces_of(slot)]

    def far(entry):
        offset = entry[0]
        return (-(2 * abs(offset[1]) + abs(offset[0])), entry)

    return slots, sorted(plan, key=far)


def kernel(sizes, links_hbm, trials_hbm, cos_hbm, azim_hbm, acc_hbm, new_hbm, trans_hbm,
           own, halo, trials, cosv, azim, acc, new, trans, total, gathered, before,
           local_sem, send_sem, recv_sem, tot_send, tot_recv):
    slots, plan = copies_of(sizes)
    me = tuple(lax.axis_index(name) for name in AXES)

    def device(offset):
        return {
            name: lax.rem(place + (step % size), size)
            for name, place, step, size in zip(AXES, me, offset, sizes)
        }

    laps = sizes[0]
    partners = list(slots)
    for lap in range(1, laps):
        key = (lap if lap < laps - 1 else -1, 0, 0)
        key = canonical(key, sizes)
        if key not in partners:
            partners.append(key)

    barrier = pltpu.get_barrier_semaphore()
    for offset in partners:
        pl.semaphore_signal(barrier, inc=1, device_id=device(offset), device_id_type=MESH)

    locals_ = [
        pltpu.make_async_copy(src, dst, local_sem.at[index])
        for index, (src, dst) in enumerate(
            ((links_hbm, own), (acc_hbm, acc), (trials_hbm, trials), (azim_hbm, azim), (cos_hbm, cosv))
        )
    ]
    for copy in locals_:
        copy.start()

    pl.semaphore_wait(barrier, len(partners))

    sends = {}
    for index, (slot, (first, stop)) in enumerate(plan):
        back = tuple(-step for step in slot)
        copy = pltpu.make_async_remote_copy(
            src_ref=links_hbm.at[pl.ds(first, stop - first)],
            dst_ref=halo.at[slots.index(slot), pl.ds(first, stop - first)],
            send_sem=send_sem.at[index],
            recv_sem=recv_sem.at[index],
            device_id=device(back),
            device_id_type=MESH,
        )
        copy.start()
        sends[(slot, first)] = copy

    rows, lanes = own.shape[2:]
    row = lax.broadcasted_iota(jnp.int32, (rows, lanes), 0)
    lane = lax.broadcasted_iota(jnp.int32, (rows, lanes), 1)
    bit = [(row // value) % 2 == 1 for value in BITS]
    even = (row // 4 + row // 2 + row + lane) % 2 == 0

    for copy in locals_:
        copy.wait()

    draws, polar, trig_cos, trig_sin = [], [], [], []
    for along in range(4):
        which = acc[along]
        draw = trials[0, along]
        for number in range(1, trials.shape[0]):
            draw = jnp.where(which == number, trials[number, along], draw)
        draws.append(draw)
        cosine = cosv[along]
        side = jnp.sqrt(1.0 - cosine * cosine)
        polar.append(cosine)
        trig_cos.append(side * jnp.cos(azim[along]))
        trig_sin.append(side * jnp.sin(azim[along]))

    arrived = set()

    def arrive(used):
        for slot, (first, stop) in plan:
            axes = {axis for axis in range(3) if slot[axis]}
            if axes <= used and (slot, first) not in arrived:
                arrived.add((slot, first))
                sends[(slot, first)].wait_recv()

    memo = {}

    def block(direction, part, blk):
        blk = canonical(blk, sizes)
        key = ("block", direction, part, blk)
        if key not in memo:
            if blk == (0, 0, 0):
                memo[key] = own[direction, part]
            else:
                memo[key] = halo[slots.index(blk), direction, part]
        return memo[key]

    def field(direction, part, blk, offset):
        blk = canonical(blk, sizes)
        key = (direction, part, blk, offset)
        if key in memo:
            return memo[key]
        if offset[3]:
            flat = field(direction, part, blk, offset[:3] + (0,))
            value = pltpu.roll(flat, (-offset[3]) % lanes, 1)
        else:
            moved = [axis for axis in range(3) if offset[axis]]
            if not moved:
                value = block(direction, part, blk)
            else:
                axis = moved[0]
                step = offset[axis]
                for other in moved:
                    if abs(offset[other]) == 2:
                        axis, step = other, offset[other]
                rest = offset[:axis] + (0,) + offset[axis + 1 :]
                sign = 1 if step > 0 else -1
                beyond = blk[:axis] + (sign,) + blk[axis + 1 :]
                far = field(direction, part, beyond, rest)
                if abs(step) == 2:
                    value = far
                else:
                    near = field(direction, part, blk, rest)
                    size = BITS[axis]
                    if size * 2 == rows:
                        mixed = jnp.where(bit[axis], near, far) if step > 0 else jnp.where(bit[axis], far, near)
                        value = pltpu.roll(mixed, size, 0)
                    elif step > 0:
                        value = jnp.where(bit[axis], pltpu.roll(far, size, 0), pltpu.roll(near, rows - size, 0))
                    else:
                        value = jnp.where(bit[axis], pltpu.roll(near, size, 0), pltpu.roll(far, rows - size, 0))
        memo[key] = value
        return value

    ending = [None] * 4
    leading = [None] * 4

    def add(store, along, value):
        value = Quat(value.plain())
        store[along] = value if store[along] is None else store[along] + value

    def pair(along, across):
        def at(direction, step_along, step_across):
            offset = [0, 0, 0, 0]
            offset[along] = step_along
            offset[across] = step_across
            return Quat(tuple(field(direction, part, (0, 0, 0), tuple(offset)) for part in range(4)))

        corner = at(across, 1, 0) * at(along, 0, 1).conj()
        wide = (at(along, 1, 0) * at(across, 2, 0)) * (at(along, 0, 1) * at(along, 1, 1)).conj()
        tall = (at(across, 1, 0) * at(across, 1, 1)) * (at(across, 0, 1) * at(along, 0, 2)).conj()
        add(ending, along, (corner.scaled(plaq_weight) + (wide + tall).scaled(rect_weight)) * at(across, 0, 0).conj())
        add(leading, along, corner * (at(across, -1, 0) * at(along, -1, 1)).conj())
        corner = (at(along, 0, -1) * at(across, 1, -1)).conj()
        wide = (at(along, 1, 0) * at(across, 2, -1).conj()) * (at(along, 0, -1) * at(along, 1, -1)).conj()
        tall = (at(across, 1, -2) * at(across, 1, -1)).conj() * (at(along, 0, -2).conj() * at(across, 0, -2))
        corner_plain = Quat(corner.plain())
        add(
            ending,
            along,
            (corner_plain.scaled(plaq_weight) + (wide + tall).scaled(rect_weight)) * at(across, 0, -1),
        )
        add(leading, along, corner * (at(along, -1, -1).conj() * at(across, -1, -1)))

    def heat_bath(along):
        offset = [0, 0, 0, 0]
        offset[along] = -1
        back = Quat(tuple(field(along, part, (0, 0, 0), tuple(offset)) for part in range(4)))
        staple = ending[along] + (leading[along] * back).scaled(rect_weight)
        s0, s1, s2, s3 = staple.parts
        size = jnp.sqrt((s0 * s0 + s1 * s1) + (s2 * s2 + s3 * s3))
        floor = jnp.maximum(size, 1.0)
        strength = coupling * floor
        low = jnp.exp(-2.0 * strength)
        head = 1.0 + jnp.log(low + (1.0 - low) * draws[along]) / strength
        radius = jnp.sqrt(1.0 - head * head)
        trial = Quat((head, radius * trig_cos[along], radius * trig_sin[along], radius * polar[along]))
        inverse = 1.0 / floor
        updated = (trial * staple.conj()).scaled(inverse)
        out = tuple(
            jnp.where(even, value, block(along, part, (0, 0, 0))) for part, value in enumerate(updated.parts)
        )
        for part in range(4):
            new[along, part] = out[part]
        return out

    arrive({2})
    pair(2, 3)
    pair(3, 2)
    arrive({0, 2})
    pair(0, 3)
    pair(0, 2)
    pair(3, 0)
    pair(2, 0)
    arrive({0, 1, 2})
    pair(0, 1)
    new_t = heat_bath(0)

    turned = tuple(pltpu.roll(part, 4, 0) for part in new_t)
    first = Quat(tuple(jnp.where(bit[0], b, a) for a, b in zip(new_t, turned)))
    second = Quat(tuple(jnp.where(bit[0], a, b) for a, b in zip(new_t, turned)))
    both = first * second
    inner = Quat(tuple(jnp.where(bit[0], b, a) for a, b in zip(first.parts, both.parts)))
    for part in range(4):
        total[part] = both.parts[part]

    def hop(lap):
        return pltpu.make_async_remote_copy(
            src_ref=total,
            dst_ref=gathered.at[lap],
            send_sem=tot_send.at[lap],
            recv_sem=tot_recv.at[lap],
            device_id=device((lap, 0, 0)),
            device_id_type=MESH,
        )

    for lap in range(laps - 1, 0, -1):

        @pl.when(me[0] + lap < laps)
        def _():
            hop(lap).start()

    for along, across in ((1, 0), (1, 2), (1, 3)):
        pair(along, across)
    heat_bath(1)
    pair(2, 1)
    heat_bath(2)
    pair(3, 1)
    heat_bath(3)
    out_new = pltpu.make_async_copy(new, new_hbm, local_sem.at[5])
    out_new.start()

    for part in range(4):
        before[part] = jnp.full((rows, lanes), 1.0 if part == 0 else 0.0, jnp.float32)
    for lap in range(laps - 1, 0, -1):

        @pl.when(me[0] >= lap)
        def _():
            hop(lap).wait_recv()
            state = Quat(tuple(before[part] for part in range(4)))
            state = state * Quat(tuple(gathered[lap, part] for part in range(4)))
            for part in range(4):
                before[part] = state.parts[part]

    final = Quat(tuple(before[part] for part in range(4))) * inner
    for part in range(4):
        trans[part] = final.parts[part]
    out_trans = pltpu.make_async_copy(trans, trans_hbm, local_sem.at[6])
    out_trans.start()

    for copy in sends.values():
        copy.wait_send()
    for lap in range(laps - 1, 0, -1):

        @pl.when(me[0] + lap < laps)
        def _():
            hop(lap).wait_send()

    out_new.wait()
    out_trans.wait()


def solution(mesh):
    sizes = tuple(mesh.shape[name] for name in AXES)

    def local(links, trials, cos_polar, azimuth, accepted):
        dirs, comps, t_len, x_len, y_len, z_len = links.shape
        assert (t_len, x_len, y_len) == (2, 2, 2)
        rows = t_len * x_len * y_len
        tile = (rows, z_len)
        slots, plan = copies_of(sizes)
        any_spec = pl.BlockSpec(memory_space=pl.ANY)
        f32 = jnp.float32

        def run(*args):
            return kernel(sizes, *args)

        new, trans = pl.pallas_call(
            run,
            out_shape=(
                jax.ShapeDtypeStruct((dirs, comps) + tile, f32),
                jax.ShapeDtypeStruct((comps,) + tile, f32),
            ),
            in_specs=[any_spec] * 5,
            out_specs=(any_spec, any_spec),
            scratch_shapes=[
                pltpu.VMEM((dirs, comps) + tile, f32),
                pltpu.VMEM((len(slots), dirs, comps) + tile, f32),
                pltpu.VMEM((trials.shape[0], dirs) + tile, f32),
                pltpu.VMEM((dirs,) + tile, f32),
                pltpu.VMEM((dirs,) + tile, f32),
                pltpu.VMEM((dirs,) + tile, jnp.int32),
                pltpu.VMEM((dirs, comps) + tile, f32),
                pltpu.VMEM((comps,) + tile, f32),
                pltpu.VMEM((comps,) + tile, f32),
                pltpu.VMEM((sizes[0], comps) + tile, f32),
                pltpu.VMEM((comps,) + tile, f32),
                pltpu.SemaphoreType.DMA((7,)),
                pltpu.SemaphoreType.DMA((len(plan),)),
                pltpu.SemaphoreType.DMA((len(plan),)),
                pltpu.SemaphoreType.DMA((sizes[0],)),
                pltpu.SemaphoreType.DMA((sizes[0],)),
            ],
            compiler_params=pltpu.CompilerParams(collective_id=0, has_side_effects=True),
        )(
            links.reshape((dirs, comps) + tile),
            trials.reshape((trials.shape[0], dirs) + tile),
            cos_polar.reshape((dirs,) + tile),
            azimuth.reshape((dirs,) + tile),
            accepted.reshape((dirs,) + tile),
        )
        return new.reshape(links.shape), trans.reshape(links.shape[1:])

    return jax.shard_map(
        local,
        mesh=mesh,
        in_specs=(
            P(None, None, "zt", "gx", "gy", None),
            P(None, None, "zt", "gx", "gy", None),
            P(None, "zt", "gx", "gy", None),
            P(None, "zt", "gx", "gy", None),
            P(None, "zt", "gx", "gy", None),
        ),
        out_specs=(P(None, None, "zt", "gx", "gy", None), P(None, "zt", "gx", "gy", None)),
        check_vma=False,
    )
```

time: 132 us -> 19.9 us (0.15)
  other arithmetic: 84.3 us -> 0 us
  Pallas kernels: 0 us -> 16.9 us
  blocking collectives: 13.1 us -> 0 us
  waiting for transfers between devices: 12.1 us -> 0 us
  starting transfers between devices: 8.68 us -> 0 us
  local copies, waits for them, and re-layouts: 7.73 us -> 2.09 us
  between operations: 4.27 us -> 0.65 us
    sub x152 -> x0, other arithmetic: 38.4 us -> none  [quat_mul(): left[0] * right[0] - left[1] * right[1] - left[2] * right[2]]
    add x131 -> x0, other arithmetic: 25 us -> none  [the longest x126 24.9 us: quat_mul(): left[0] * right[1] + right[0] * left[1] - left[2] * right[3]]
    pallas_call x0 -> x1, Pallas kernels: none -> 16.9 us  [local(): pl.pallas_call(run, out_shape=(jax.ShapeDtypeStruct((dirs, comps) + tile,...]
    all_gather x1 -> x0, blocking collectives: 13.1 us -> none  [entering(): gathered = lax.all_gather(part, axis)]
    ppermute x6 -> x0, waiting for transfers between devices: 12.1 us -> none  [the longest x3 11.4 us: with_halo(): before = lax.ppermute(last, axis, up)]
    neg x69 -> x0, other arithmetic: 10.8 us -> none  [quat_conj(): return jnp.concatenate([value[:1], -value[1:]], axis=0)]
    ppermute x6 -> x0, starting transfers between devices: 8.68 us -> none  [the longest x3 5.59 us: with_halo(): after = lax.ppermute(leading, axis, down)]
    slice x43 -> x0, local copies, waits for them, and re-layouts: 5.19 us -> none  [the longest x41 5.19 us: lookup(): memo[keyname] = jnp.roll(piece, -offset[3], axis=4)]
  transfers between devices with their start and end apart: 6 -> 0, of which waited for: 2 -> 0; matrix products, arithmetic and copies ran while one was open for 24% -> 0% of each run, Pallas kernels for 0% -> 0%
where the time goes in v1:
time: 19.9 us; the launch traced here: 19.6 us
  Pallas kernels  16.9 us (85%)
  local copies, waits for them, and re-layouts  2.09 us (11%)
  between operations  0.65 us (3%)
    pallas_call x1, Pallas kernels, local(): pl.pallas_call(run, out_shape=(jax.ShapeDtypeStruct((dirs, comps) + tile,...  16.9 us
    unnamed x4, local copies, waits for them, and re-layouts  2.09 us

profile of v1, /device:TPU:0, one launch (start us, length us, event | category | flops | bytes accessed | tf_op | source)
XLA Modules:
  0.0 19.6 jit_solution(7040811911403053384)
XLA Ops:
  0.6 16.9 %shard_map.68 = (f32[4,4,8,128]{3,2,1,0:T(8,128)}, f32[4,8,128]{2,1,0:T(8,128)}) custom-call(f32[4,4,8,128]{3,2,1,0:T(8,128)} %bitcast.9, f32[8,4,8,128]{3,2,1,0:T(8,128)} %bitcast.7, f32[4,8,128]{2,1,0:T(8,128)} %bitcast.11, f32[4,8,128]{2,1,0:T(8,128)} %bitcast.12, s32[4,8,128]{2,1,0:T(8,128)} %bitcast.13), custom_call_target="tpu_custom_call" | custom-call | tf_op jit(solution)/shard_map/pallas_call | solution.py:382
  17.5 0.0 copy-start
  17.5 1.5 %copy.9 = f32[4,4,2,2,2,128]{5,4,3,2,1,0:T(2,128)} copy(f32[4,4,2,2,2,128]{5,4,3,2,1,0:T(2,128)} %bitcast.8) | data formatting | bytes 131072
  19.0 0.0 copy-done
  19.0 0.6 %copy.10 = f32[4,2,2,2,128]{4,3,2,1,0:T(2,128)} copy(f32[4,2,2,2,128]{4,3,2,1,0:T(2,128)S(1)} %bitcast.10) | data formatting | bytes 32768
Async XLA Ops:
  17.5 1.5 %copy-start = (f32[4,8,128]{2,1,0:T(8,128)S(1)}, f32[4,8,128]{2,1,0:T(8,128)}, u32[]{:S(2)}) copy-start(f32[4,8,128]{2,1,0:T(8,128)} %get-tuple-element.5) | copy-start | bytes 49156

commit v2 on v1

--- a/solution.py
+++ b/solution.py
@@ -86,19 +86,41 @@
     return slots
 
 
-def pieces_of(offset):
+def pieces_of(offset, sizes):
     used = [axis for axis in range(3) if offset[axis]]
     if len(used) == 1:
-        return ((0, 4),)
+        return (((0, 4), (0, 8)),)
     low, high = used
-    if high == low + 1:
-        return ((low, high + 1),)
-    return ((low, low + 1), (high, high + 1))
+    both = sizes[high] == 2
+    ends = {low: 0 if offset[low] > 0 else 1}
+    if not both:
+        ends[high] = 0 if offset[high] > 0 else 1
+    rows = [
+        row for row in range(8) if all((row // BITS[axis]) % 2 == end for axis, end in ends.items())
+    ]
+    runs = []
+    for row in rows:
+        if runs and runs[-1][0] + runs[-1][1] == row:
+            runs[-1][1] += 1
+        else:
+            runs.append([row, 1])
+    whole = set()
+    if offset[low] > 0 and (both or offset[high] < 0):
+        whole.add(high)
+    if offset[low] < 0 and (both or offset[high] > 0):
+        whole.add(low)
+    if not whole and high == low + 1:
+        return tuple(((low, 2), tuple(run)) for run in runs)
+    pieces = []
+    for axis in used:
+        for run in [(0, 8)] if axis in whole else runs:
+            pieces.append(((axis, 1), tuple(run)))
+    return tuple(pieces)
 
 
 def copies_of(sizes):
     slots = halo_slots(sizes)
-    plan = [(slot, piece) for slot in slots for piece in pieces_of(slot)]
+    plan = [(slot, piece) for slot in slots for piece in pieces_of(slot, sizes)]
 
     def far(entry):
         offset = entry[0]
@@ -107,8 +129,8 @@
     return slots, sorted(plan, key=far)
 
 
-def kernel(sizes, links_hbm, trials_hbm, cos_hbm, azim_hbm, acc_hbm, new_hbm, trans_hbm,
-           own, halo, trials, cosv, azim, acc, new, trans, total, gathered, before,
+def kernel(sizes, links_hbm, trials_hbm, cos_hbm, azim_hbm, acc_hbm, new, trans,
+           own, halo, trials, cosv, azim, acc, total, gathered, before,
            local_sem, send_sem, recv_sem, tot_send, tot_recv):
     slots, plan = copies_of(sizes)
     me = tuple(lax.axis_index(name) for name in AXES)
@@ -143,18 +165,19 @@
     pl.semaphore_wait(barrier, len(partners))
 
     sends = {}
-    for index, (slot, (first, stop)) in enumerate(plan):
+    for index, (slot, piece) in enumerate(plan):
+        (first, count), (start, length) = piece
         back = tuple(-step for step in slot)
         copy = pltpu.make_async_remote_copy(
-            src_ref=links_hbm.at[pl.ds(first, stop - first)],
-            dst_ref=halo.at[slots.index(slot), pl.ds(first, stop - first)],
+            src_ref=links_hbm.at[pl.ds(first, count), :, pl.ds(start, length)],
+            dst_ref=halo.at[slots.index(slot), pl.ds(first, count), :, pl.ds(start, length)],
             send_sem=send_sem.at[index],
             recv_sem=recv_sem.at[index],
             device_id=device(back),
             device_id_type=MESH,
         )
         copy.start()
-        sends[(slot, first)] = copy
+        sends[(slot, piece)] = copy
 
     rows, lanes = own.shape[2:]
     row = lax.broadcasted_iota(jnp.int32, (rows, lanes), 0)
@@ -181,11 +204,11 @@
     arrived = set()
 
     def arrive(used):
-        for slot, (first, stop) in plan:
+        for slot, piece in plan:
             axes = {axis for axis in range(3) if slot[axis]}
-            if axes <= used and (slot, first) not in arrived:
-                arrived.add((slot, first))
-                sends[(slot, first)].wait_recv()
+            if axes <= used and (slot, piece) not in arrived:
+                arrived.add((slot, piece))
+                sends[(slot, piece)].wait_recv()
 
     memo = {}
 
@@ -331,8 +354,6 @@
     heat_bath(2)
     pair(3, 1)
     heat_bath(3)
-    out_new = pltpu.make_async_copy(new, new_hbm, local_sem.at[5])
-    out_new.start()
 
     for part in range(4):
         before[part] = jnp.full((rows, lanes), 1.0 if part == 0 else 0.0, jnp.float32)
@@ -349,8 +370,6 @@
     final = Quat(tuple(before[part] for part in range(4))) * inner
     for part in range(4):
         trans[part] = final.parts[part]
-    out_trans = pltpu.make_async_copy(trans, trans_hbm, local_sem.at[6])
-    out_trans.start()
 
     for copy in sends.values():
         copy.wait_send()
@@ -359,9 +378,6 @@
         @pl.when(me[0] + lap < laps)
         def _():
             hop(lap).wait_send()
-
-    out_new.wait()
-    out_trans.wait()
 
 
 def solution(mesh):
@@ -382,11 +398,11 @@
         new, trans = pl.pallas_call(
             run,
             out_shape=(
-                jax.ShapeDtypeStruct((dirs, comps) + tile, f32),
-                jax.ShapeDtypeStruct((comps,) + tile, f32),
+                pltpu.VMEM((dirs, comps) + tile, f32),
+                pltpu.VMEM((comps,) + tile, f32),
             ),
             in_specs=[any_spec] * 5,
-            out_specs=(any_spec, any_spec),
+            out_specs=(pl.BlockSpec(memory_space=pltpu.VMEM),) * 2,
             scratch_shapes=[
                 pltpu.VMEM((dirs, comps) + tile, f32),
                 pltpu.VMEM((len(slots), dirs, comps) + tile, f32),
@@ -394,12 +410,10 @@
                 pltpu.VMEM((dirs,) + tile, f32),
                 pltpu.VMEM((dirs,) + tile, f32),
                 pltpu.VMEM((dirs,) + tile, jnp.int32),
-                pltpu.VMEM((dirs, comps) + tile, f32),
-                pltpu.VMEM((comps,) + tile, f32),
                 pltpu.VMEM((comps,) + tile, f32),
                 pltpu.VMEM((sizes[0], comps) + tile, f32),
                 pltpu.VMEM((comps,) + tile, f32),
-                pltpu.SemaphoreType.DMA((7,)),
+                pltpu.SemaphoreType.DMA((5,)),
                 pltpu.SemaphoreType.DMA((len(plan),)),
                 pltpu.SemaphoreType.DMA((len(plan),)),
                 pltpu.SemaphoreType.DMA((sizes[0],)),

time: 19.9 us -> 17.3 us (0.87)
  Pallas kernels: 16.9 us -> 15.3 us
  local copies, waits for them, and re-layouts: 2.09 us -> 1.24 us
    pallas_call x1, Pallas kernels: 16.9 us -> 15.3 us  [local(): pl.pallas_call(run, out_shape=(pltpu.VMEM((dirs, comps) + tile, f32), plt...]
    unnamed x4 -> x2, local copies, waits for them, and re-layouts: 2.09 us -> 1.24 us
where the time goes in v2:
time: 17.3 us; the launch traced here: 17.2 us
  Pallas kernels  15.3 us (88%)
  local copies, waits for them, and re-layouts  1.24 us (7%)
  between operations  0.64 us (4%)
    pallas_call x1, Pallas kernels, local(): pl.pallas_call(run, out_shape=(pltpu.VMEM((dirs, comps) + tile, f32), plt...  15.3 us
    unnamed x2, local copies, waits for them, and re-layouts  1.24 us

profile of v2, /device:TPU:0, one launch (start us, length us, event | category | flops | bytes accessed | tf_op | source)
XLA Modules:
  0.0 17.2 jit_solution(684358433181896303)
XLA Ops:
  0.6 15.3 %shard_map.68 = (f32[4,4,8,128]{3,2,1,0:T(8,128)S(1)}, f32[4,8,128]{2,1,0:T(8,128)S(1)}) custom-call(f32[4,4,8,128]{3,2,1,0:T(8,128)} %bitcast.10, f32[8,4,8,128]{3,2,1,0:T(8,128)} %bitcast.9, f32[4,8,128]{2,1,0:T(8,128)} %bitcast.11, f32[4,8,128]{2,1,0:T(8,128)} %bitcast.12, s32[4,8,128]{2,1,0:T(8,128)} %bitcast.13), custom_call_target="tpu_custom_call" | custom-call | tf_op jit(solution)/shard_map/pallas_call | solution.py:398
  15.9 0.6 %copy.9 = f32[4,4,2,2,2,128]{5,4,3,2,1,0:T(2,128)} copy(f32[4,4,2,2,2,128]{5,4,3,2,1,0:T(2,128)S(1)} %bitcast.7) | data formatting | bytes 131072
  16.6 0.6 %copy.10 = f32[4,2,2,2,128]{4,3,2,1,0:T(2,128)} copy(f32[4,2,2,2,128]{4,3,2,1,0:T(2,128)S(1)} %bitcast.8) | data formatting | bytes 32768
